TPU v7x, 32 devices: a whole 2x2x4 slice. The times are simulated.
32 devices in a mesh: pipe: 4 (over x, core), dp: 8 (over z, y).
Axes of the slice: x: 2, y: 2, z: 4, core: 2. Of those that a mesh axis runs over, the one named last changes fastest.
Arguments:
- section_input: bfloat16 [4, 2048, 2048], P('pipe', 'dp'), may hold values from -6 to 6
- top_grad: bfloat16 [2048, 2048], P('dp'), may hold values from -6 to 6
- w_in: bfloat16 [4, 2048, 3072], P('pipe', 'dp'), may hold values from -0.125 to 0.125
- w_out: bfloat16 [4, 1024, 2048], P('pipe', 'dp'), may hold values from -0.1875 to 0.1875
- segments: int32 [16, 128], P('dp'), may hold values from 0 to 3, never falling along the last dimension, each value on 1 to 64 neighbouring positions
Outputs:
- section_grads: bfloat16 [4, 2048, 2048], P('pipe', 'dp')
- w_in_grad: float32 [4, 2048, 3072], P('pipe', 'dp')
- w_out_grad: float32 [4, 1024, 2048], P('pipe', 'dp')
Inputs may be any that keep to these rules, and one draw needn't show every extreme that they name: `segments`: in every row the history numbers run 0 to 3 without falling, each history has 1 to 64 positions, and one has exactly 64.
All inputs are finite; a program needn't handle non-finite values.
Results may differ from a plain program's by a relative error of at most 0.03.
Values may be sent and summed in bfloat16 or wider, within the bound.
A program may use at most 128 MiB of HBM per device.

v0:
```python
import jax
import jax.numpy as jnp
from jax import lax
from jax.sharding import PartitionSpec as P

HEADS = 16
QK_DIM = 32
V_DIM = 64
EPSILON = 1e-05


def passed_along(shard, axis, by):
    devices = lax.axis_size(axis)
    pairs = [(i, i + by) for i in range(devices) if 0 <= i + by < devices]
    return lax.ppermute(shard, axis, pairs)


def norm_rows(values):
    center = values - jnp.mean(values, axis=-1, keepdims=True)
    return center * lax.rsqrt(jnp.mean(center * center, axis=-1, keepdims=True) + EPSILON)


def silu_slope(preact):
    squash = jax.nn.sigmoid(preact)
    return squash * (1.0 + preact * (1.0 - squash))


def contract_rows(left, right):
    return lax.dot_general(
        left, right, (((0,), (0,)), ((), ())), preferred_element_type=jnp.float32
    )


def forward_front(inputs, w_first):
    normed = norm_rows(inputs.astype(jnp.float32)).astype(jnp.bfloat16)
    preact = jnp.dot(normed, w_first, preferred_element_type=jnp.float32)
    return (normed, preact, jax.nn.silu(preact).astype(jnp.bfloat16))


def attend(activated, history):
    row_count = activated.shape[0]
    value_cols = HEADS * V_DIM
    query_cols = HEADS * QK_DIM
    active32 = activated.astype(jnp.float32)
    gating = active32[:, :value_cols]
    values = active32[:, value_cols : 2 * value_cols].reshape(row_count, HEADS, V_DIM)
    queries = active32[:, 2 * value_cols : 2 * value_cols + query_cols].reshape(
        row_count, HEADS, QK_DIM
    )
    key_rows = active32[:, 2 * value_cols + query_cols :].reshape(row_count, HEADS, QK_DIM)
    scores = jnp.einsum("qhd,khd->hqk", queries, key_rows) * QK_DIM ** (-0.5)
    same_doc = history[:, None] == history[None, :]
    positions = lax.broadcasted_iota(jnp.int32, (row_count, row_count), 0)
    columns = lax.broadcasted_iota(jnp.int32, (row_count, row_count), 1)
    allowed = jnp.logical_and(same_doc, columns <= positions)
    counts = jnp.sum(same_doc.astype(jnp.float32), axis=1)
    weights_mask = allowed.astype(jnp.float32) / counts[:, None]
    weights = jax.nn.silu(scores) * weights_mask[None]
    mixed = jnp.einsum("hqk,khd->qhd", weights, values).reshape(row_count, value_cols)
    return norm_rows(mixed) * gating


def layer_back(inputs, preact, activated, upstream, history, w_first, w_second):
    gated_full, pull = jax.vjp(lambda active_in: attend(active_in, history), activated)
    gated = gated_full.astype(jnp.bfloat16)
    grad_second = contract_rows(gated, upstream)
    grad_gated = lax.dot_general(
        upstream, w_second, (((1,), (1,)), ((), ())), preferred_element_type=jnp.float32
    )
    (grad_active,) = pull(grad_gated)
    grad_preact = (grad_active.astype(jnp.float32) * silu_slope(preact)).astype(jnp.bfloat16)
    grad_normed = lax.dot_general(
        grad_preact, w_first, (((1,), (1,)), ((), ())), preferred_element_type=jnp.float32
    )
    _, pull_norm = jax.vjp(norm_rows, inputs.astype(jnp.float32))
    (grad_through,) = pull_norm(grad_normed)
    grad_input = (upstream.astype(jnp.float32) + grad_through).astype(jnp.bfloat16)
    return (grad_input, grad_preact, grad_second)


def body(section_input, top_grad, w_in, w_out, segments):
    w_first = lax.all_gather(w_in[0], "dp", axis=0, tiled=True)
    w_second = lax.all_gather(w_out[0], "dp", axis=0, tiled=True)
    sections = lax.axis_size("pipe")
    section = lax.axis_index("pipe")
    inputs_all = section_input[0]
    micro = segments.shape[0]
    length = segments.shape[1]
    width = inputs_all.shape[1]
    hidden_cols = w_first.shape[1]
    store = jnp.zeros((micro * length, hidden_cols), jnp.bfloat16)

    def one_step(step_index, carry):
        incoming, store_now, acc_out, grads = carry
        slot = step_index - (sections - 1 - section)
        active = jnp.logical_and(slot >= 0, slot < micro)
        slot = jnp.clip(slot, 0, micro - 1)
        start = slot * length
        top_rows = lax.dynamic_slice_in_dim(top_grad, start, length, 0)
        upstream = jnp.where(section == sections - 1, top_rows, incoming)
        history = lax.dynamic_index_in_dim(segments, slot, 0, keepdims=False)

        def work():
            inputs = lax.dynamic_slice_in_dim(inputs_all, start, length, 0)
            normed, preact, activated = forward_front(inputs, w_first)
            grad_input, grad_preact, grad_second = layer_back(
                inputs, preact, activated, upstream, history, w_first, w_second
            )
            store_next = lax.dynamic_update_slice_in_dim(store_now, grad_preact, start, 0)
            grads_next = lax.dynamic_update_slice_in_dim(grads, grad_input, start, 0)
            return (grad_input, store_next, acc_out + grad_second, grads_next)

        def resting():
            return (jnp.zeros_like(incoming), store_now, acc_out, grads)

        outgoing, store_now, acc_out, grads = lax.cond(active, work, resting)
        incoming = passed_along(outgoing, "pipe", -1)
        return (incoming, store_now, acc_out, grads)

    start_carry = (
        jnp.zeros((length, width), jnp.bfloat16),
        store,
        jnp.zeros((w_second.shape[0], width), jnp.float32),
        jnp.zeros_like(inputs_all),
    )
    _, store, acc_out, grads = lax.fori_loop(0, sections + micro - 1, one_step, start_carry)
    normed_rows = norm_rows(inputs_all.astype(jnp.float32)).astype(jnp.bfloat16)
    grad_first = lax.psum_scatter(
        contract_rows(normed_rows, store).astype(jnp.bfloat16),
        "dp",
        scatter_dimension=0,
        tiled=True,
    ).astype(jnp.float32)
    grad_out = lax.psum_scatter(
        acc_out.astype(jnp.bfloat16), "dp", scatter_dimension=0, tiled=True
    ).astype(jnp.float32)
    return (grads[None], grad_first[None], grad_out[None])


def solution(mesh):
    return jax.shard_map(
        body,
        mesh=mesh,
        in_specs=(
            P("pipe", "dp", None),
            P("dp", None),
            P("pipe", "dp", None),
            P("pipe", "dp", None),
            P("dp", None),
        ),
        out_specs=(P("pipe", "dp", None), P("pipe", "dp", None), P("pipe", "dp", None)),
        check_vma=False,
    )
```

profile of v0, /device:TPU:0, one launch (start us, length us, event | category | flops | bytes accessed | tf_op | source)
XLA Modules:
  0.0 868.3 jit_solution(9166335217495823203)
XLA Ops:
  8.7 76.9 %all-gather.5.cloned.1.call-done = bf16[1,1024,2048]{2,1,0:T(8,128)(2,1)} async-done(((bf16[1,128,2048]{2,1,0:T(8,128)(2,1)}), bf16[1,1024,2048]{2,1,0:T(8,128)(2,1)}) %all-gather.5.cloned.1.call-update) | async-done | bytes 4194320 | tf_op jit(solution)/shard_map/all_gather | solution.py:83
  85.6 176.9 %all-gather.7.cloned.1.call-done = bf16[1,2048,3072]{2,1,0:T(8,128)(2,1)} async-done(((bf16[1,256,3072]{2,1,0:T(8,128)(2,1)}), bf16[1,2048,3072]{2,1,0:T(8,128)(2,1)}) %all-gather.7.cloned.1.call-update) | async-done | bytes 12582928 | tf_op jit(solution)/shard_map/all_gather | solution.py:82
  264.7 4.3 broadcast_in_dim.57
  270.0 285.4 %while.21 = (s32[]{:T(128)}, bf16[128,2048]{1,0:T(8,128)(2,1)}, bf16[256,3072]{1,0:T(8,128)(2,1)}, f32[1024,2048]{1,0:T(8,128)}, bf16[256,2048]{1,0:T(8,128)(2,1...) while((s32[]{:T(128)}, bf16[128,2048]{1,0:T(8,128)(2,1)}, ...), condition=%wide.region_12.13_spmd, body=%wide.region_0.12_spmd.sunk | while | flops 4473488384 | bytes 157841232 | solution.py:126
  277.8 8.8 %collective-permute-done = bf16[128,2048]{1,0:T(8,128)(2,1)S(1)} collective-permute-done((bf16[128,2048]{1,0:T(8,128)(2,1)}, bf16[128,2048]{1,0:T(8,128)(2,1)S(1)}, u32[]{:S(2)}, u32[]{:S(2)}) %collective-permute-start) | collective-permute-done | bytes 524320 | tf_op jit(solution)/shard_map/while/body/eval_jaxpr/ppermute | solution.py:15
  289.5 148.4 %collective-permute-done = bf16[128,2048]{1,0:T(8,128)(2,1)S(1)} collective-permute-done((bf16[128,2048]{1,0:T(8,128)(2,1)}, bf16[128,2048]{1,0:T(8,128)(2,1)S(1)}, u32[]{:S(2)}, u32[]{:S(2)}) %collective-permute-start) | collective-permute-done | bytes 524320 | tf_op jit(solution)/shard_map/while/body/eval_jaxpr/ppermute | solution.py:15
  438.8 50.1 %conditional.2 = (bf16[128,2048]{1,0:T(8,128)(2,1)}, bf16[256,3072]{1,0:T(8,128)(2,1)}, f32[1024,2048]{1,0:T(8,128)}, bf16[256,2048]{1,0:T(8,128)(2,1)}) conditional(s32[]{:T(128)} %convert_element_type.154, (bf16[256,3072]{1,0:T(8,128)(2,1)}, f32[1024,2048]{1,0:T(8,128)}, bf16[256,2048]{1,0:T(8,128)(2,1)}) %tuple.69, (pred[]{:T(512)}, s32[]{:T(128)}, ...), branch_computations={%region_1.1_spmd, %region_2.11_spmd} | conditional | flops 4473488384 | bytes 153646560 | solution.py:116
  439.3 7.9 multiply_convert_fusion.1
  451.2 3.8 multiply_reduce_fusion
  469.9 3.2 constant_dynamic-update-slice_fusion
  473.1 9.0 %fusion.6 = (f32[128]{0:T(128)S(1)}, f32[128,2048]{1,0:T(8,128)S(1)}) fusion(f32[128]{0:T(128)S(1)} %broadcast_multiply_fusion.1, bf16[256,2048]{1,0:T(8,128)(2,1)S(1)} %get-tuple-element.374, s32[]{:T(128)S(6)} %select_n.43, bf16[128,3072]{1,0:T(8,128)(2,1)S(1)} %get-tuple-element.433, bf16[2048,3072]{1,0:T(8,128)(2,1)} %get-tuple-element.375), kind=kOutput, calls=%fused_computation.17 | convolution fusion | flops 1611661184 | bytes 14943236 | tf_op jit(solution)/shard_map/while/body/eval_jaxpr/cond/branch_1_fun/dot_general | solution.py:72
  485.7 3.2 copy-done
  490.2 9.4 %collective-permute-done = bf16[128,2048]{1,0:T(8,128)(2,1)S(1)} collective-permute-done((bf16[128,2048]{1,0:T(8,128)(2,1)}, bf16[128,2048]{1,0:T(8,128)(2,1)S(1)}, u32[]{:S(2)}, u32[]{:S(2)}) %collective-permute-start) | collective-permute-done | bytes 524320 | tf_op jit(solution)/shard_map/while/body/eval_jaxpr/ppermute | solution.py:15
  500.4 50.1 %conditional.2 = (bf16[128,2048]{1,0:T(8,128)(2,1)}, bf16[256,3072]{1,0:T(8,128)(2,1)}, f32[1024,2048]{1,0:T(8,128)}, bf16[256,2048]{1,0:T(8,128)(2,1)}) conditional(s32[]{:T(128)} %convert_element_type.154, (bf16[256,3072]{1,0:T(8,128)(2,1)}, f32[1024,2048]{1,0:T(8,128)}, bf16[256,2048]{1,0:T(8,128)(2,1)}) %tuple.69, (pred[]{:T(512)}, s32[]{:T(128)}, ...), branch_computations={%region_1.1_spmd, %region_2.11_spmd} | conditional | flops 4473488384 | bytes 153646560 | solution.py:116
  500.9 7.9 multiply_convert_fusion.1
  512.9 3.8 multiply_reduce_fusion
  531.5 3.2 constant_dynamic-update-slice_fusion
  534.8 9.0 %fusion.6 = (f32[128]{0:T(128)S(1)}, f32[128,2048]{1,0:T(8,128)S(1)}) fusion(f32[128]{0:T(128)S(1)} %broadcast_multiply_fusion.1, bf16[256,2048]{1,0:T(8,128)(2,1)S(1)} %get-tuple-element.374, s32[]{:T(128)S(6)} %select_n.43, bf16[128,3072]{1,0:T(8,128)(2,1)S(1)} %get-tuple-element.433, bf16[2048,3072]{1,0:T(8,128)(2,1)} %get-tuple-element.375), kind=kOutput, calls=%fused_computation.17 | convolution fusion | flops 1611661184 | bytes 14943236 | tf_op jit(solution)/shard_map/while/body/eval_jaxpr/cond/branch_1_fun/dot_general | solution.py:72
  547.4 3.2 copy-done
  555.4 6.0 convert_element_type.89
  562.1 8.0 convolution_convert_fusion
  570.2 77.7 %reduce-scatter.5.cloned.1.call-done = bf16[128,2048]{1,0:T(8,128)(2,1)} async-done(((bf16[1024,2048]{1,0:T(8,128)(2,1)}), bf16[128,2048]{1,0:T(8,128)(2,1)}) %reduce-scatter.5.cloned.1.call-update) | async-done | bytes 524304 | tf_op jit(solution)/shard_map/reduce_scatter | solution.py:134
  650.0 208.4 %reduce-scatter.3.cloned.1.call-done = bf16[256,3072]{1,0:T(8,128)(2,1)} async-done(((bf16[2048,3072]{1,0:T(8,128)(2,1)}), bf16[256,3072]{1,0:T(8,128)(2,1)}) %reduce-scatter.3.cloned.1.call-update) | async-done | bytes 1572880 | tf_op jit(solution)/shard_map/reduce_scatter | solution.py:128
  858.4 3.4 bitcast_convert_fusion
  (159 shorter events, 74.1 us)
Async XLA Ops:
  7.2 78.5 %all-gather.5.cloned.1.call-start = ((), (), s32[]{:S(2)}) async-start(), calls=%async_computation.4 | async-start | bytes 4718592 | tf_op jit(solution)/shard_map/all_gather | solution.py:83
  7.9 254.6 %all-gather.7.cloned.1.call-start = ((), (), s32[]{:S(2)}) async-start(), calls=%async_computation.5 | async-start | bytes 14155776 | tf_op jit(solution)/shard_map/all_gather | solution.py:82
  8.6 639.2 %reduce-scatter.5.cloned.1.call-start = ((), (), s32[]{:S(2)}) async-start(), calls=%async_computation.3 | async-start | bytes 4718592 | tf_op jit(solution)/shard_map/reduce_scatter | solution.py:134
  264.7 5.4 copy-start.1
  270.9 4.0 collective-permute-start
  276.5 10.1 %collective-permute-start = (bf16[128,2048]{1,0:T(8,128)(2,1)}, bf16[128,2048]{1,0:T(8,128)(2,1)S(1)}, u32[]{:S(2)}, u32[]{:S(2)}) collective-permute-start(bf16[128,2048]{1,0:T(8,128)(2,1)} %get-tuple-element.526), channel_id=1, source_target_pairs={{8,0},{16,8},{24,16},{9,1},{17,9},{25,17},{10,2},{18,10},{26,18},{... | collective-permute-start | bytes 1572872 | tf_op jit(solution)/shard_map/while/body/eval_jaxpr/ppermute | solution.py:15
  288.3 149.7 %collective-permute-start = (bf16[128,2048]{1,0:T(8,128)(2,1)}, bf16[128,2048]{1,0:T(8,128)(2,1)S(1)}, u32[]{:S(2)}, u32[]{:S(2)}) collective-permute-start(bf16[128,2048]{1,0:T(8,128)(2,1)} %get-tuple-element.526), channel_id=1, source_target_pairs={{8,0},{16,8},{24,16},{9,1},{17,9},{25,17},{10,2},{18,10},{26,18},{... | collective-permute-start | bytes 1572872 | tf_op jit(solution)/shard_map/while/body/eval_jaxpr/ppermute | solution.py:15
  439.2 7.9 copy-start.10
  456.5 2.6 copy-start.8
  460.3 2.9 copy-start.4
  469.9 14.1 %slice-start = ((s8[8388608]{0:T(1024)(128)(4,1)}), s8[4194304]{0:T(1024)(128)(4,1)S(1)}, s32[]{:S(2)}) async-start(s8[8388608]{0:T(1024)(128)(4,1)} %bitcast.58), calls=%async_computation.6 | async-start | bytes 8388608 | tf_op jit(solution)/shard_map/while/body/eval_jaxpr/cond
  473.1 9.0 %copy-start.11 = (f32[128]{0:T(128)S(1)}, f32[128]{0:T(128)}, u32[]{:S(2)}) copy-start(f32[128]{0:T(128)} %copy-done.10) | copy-start | bytes 1540 | tf_op jit(solution)/shard_map/while/body/eval_jaxpr/cond
  473.1 10.9 %slice-start.1 = ((s8[8388608]{0:T(1024)(128)(4,1)}), s8[4194304]{0:T(1024)(128)(4,1)S(1)}, s32[]{:S(2)}) async-start(s8[8388608]{0:T(1024)(128)(4,1)} %bitcast.58), calls=%async_computation.7 | async-start | bytes 8388608 | tf_op jit(solution)/shard_map/while/body/eval_jaxpr/cond
  485.7 3.2 copy-start
  488.9 10.7 %collective-permute-start = (bf16[128,2048]{1,0:T(8,128)(2,1)}, bf16[128,2048]{1,0:T(8,128)(2,1)S(1)}, u32[]{:S(2)}, u32[]{:S(2)}) collective-permute-start(bf16[128,2048]{1,0:T(8,128)(2,1)} %get-tuple-element.526), channel_id=1, source_target_pairs={{8,0},{16,8},{24,16},{9,1},{17,9},{25,17},{10,2},{18,10},{26,18},{... | collective-permute-start | bytes 1572872 | tf_op jit(solution)/shard_map/while/body/eval_jaxpr/ppermute | solution.py:15
  500.9 7.9 copy-start.10
  518.1 2.6 copy-start.8
  522.0 2.9 copy-start.4
  531.5 14.1 %slice-start = ((s8[8388608]{0:T(1024)(128)(4,1)}), s8[4194304]{0:T(1024)(128)(4,1)S(1)}, s32[]{:S(2)}) async-start(s8[8388608]{0:T(1024)(128)(4,1)} %bitcast.58), calls=%async_computation.6 | async-start | bytes 8388608 | tf_op jit(solution)/shard_map/while/body/eval_jaxpr/cond
  534.8 9.0 %copy-start.11 = (f32[128]{0:T(128)S(1)}, f32[128]{0:T(128)}, u32[]{:S(2)}) copy-start(f32[128]{0:T(128)} %copy-done.10) | copy-start | bytes 1540 | tf_op jit(solution)/shard_map/while/body/eval_jaxpr/cond
  534.8 10.9 %slice-start.1 = ((s8[8388608]{0:T(1024)(128)(4,1)}), s8[4194304]{0:T(1024)(128)(4,1)S(1)}, s32[]{:S(2)}) async-start(s8[8388608]{0:T(1024)(128)(4,1)} %bitcast.58), calls=%async_computation.7 | async-start | bytes 8388608 | tf_op jit(solution)/shard_map/while/body/eval_jaxpr/cond
  547.4 3.2 copy-start
  550.6 4.0 collective-permute-start
  561.4 296.9 %reduce-scatter.3.cloned.1.call-start = ((), (), s32[]{:S(2)}) async-start(), calls=%async_computation.2 | async-start | bytes 14155776 | tf_op jit(solution)/shard_map/reduce_scatter | solution.py:128
  (15 other events, 18.2 us)
Sparse Core Ops, SparseCore 0:
  10.1 75.5 all-gather.4
  87.8 174.6 all-gather.6
  561.5 86.2 reduce-scatter.4
  651.3 207.0 reduce-scatter.2
where the time goes:
time: 869 us; the launch traced here: 868 us
  waiting for transfers between devices  713 us (82%)
  matrix products  70 us (8%)
  local copies, waits for them, and re-layouts  35.1 us (4%)
  other arithmetic  29.1 us (3%)
  between operations  13.8 us (2%)
    reduce_scatter x1, waiting for transfers between devices, body(): lax.psum_scatter(contract_rows(normed_rows, store).astype(jnp.bfloat16),...  208 us
    all_gather x1, waiting for transfers between devices, body(): w_first = lax.all_gather(w_in[0], 'dp', axis=0, tiled=True)  177 us
    ppermute x5, waiting for transfers between devices, passed_along(): return lax.ppermute(shard, axis, pairs)  172 us
    reduce_scatter x1, waiting for transfers between devices, body(): lax.psum_scatter(acc_out.astype(jnp.bfloat16), 'dp', scatter_dimension=0,...  77.7 us
    all_gather x1, waiting for transfers between devices, body(): w_second = lax.all_gather(w_out[0], 'dp', axis=0, tiled=True)  76.9 us
    dot_general x2, matrix products, layer_back(): lax.dot_general(grad_preact, w_first, (((1,), (1,)), ((), ())), preferred...  18.1 us
  transfers between devices with their start and end apart: 9, of which 9 were waited for; matrix products, arithmetic and copies ran while one was open for 1% of the time, Pallas kernels for 0%

commit v1 on v0

--- a/solution.py
+++ b/solution.py
@@ -7,6 +7,22 @@
 QK_DIM = 32
 V_DIM = 64
 EPSILON = 1e-05
+
+
+def ring_gather(x, axis, dim):
+    ways, here, lap = (lax.axis_size(axis), lax.axis_index(axis), x.shape[dim])
+    shape = [n * ways if d == dim else n for d, n in enumerate(x.shape)]
+    full = lax.dynamic_update_slice_in_dim(jnp.zeros(shape, x.dtype), x, here * lap, axis=dim)
+    going_up = going_down = x
+    for far in range(1, ways // 2 + 1):
+        going_up = lax.ppermute(going_up, axis, [(d, (d + 1) % ways) for d in range(ways)])
+        full = lax.dynamic_update_slice_in_dim(full, going_up, (here - far) % ways * lap, axis=dim)
+        if 2 * far < ways:
+            going_down = lax.ppermute(going_down, axis, [(d, (d - 1) % ways) for d in range(ways)])
+            full = lax.dynamic_update_slice_in_dim(
+                full, going_down, (here + far) % ways * lap, axis=dim
+            )
+    return full
 
 
 def passed_along(shard, axis, by):
@@ -80,7 +96,7 @@
 
 def body(section_input, top_grad, w_in, w_out, segments):
     w_first = lax.all_gather(w_in[0], "dp", axis=0, tiled=True)
-    w_second = lax.all_gather(w_out[0], "dp", axis=0, tiled=True)
+    w_second = ring_gather(w_out[0], "dp", 0)
     sections = lax.axis_size("pipe")
     section = lax.axis_index("pipe")
     inputs_all = section_input[0]

time: 869 us -> 830 us (0.955)
  waiting for transfers between devices: 713 us -> 648 us
  starting transfers between devices: 6.55 us -> 22.6 us
  local copies, waits for them, and re-layouts: 35.1 us -> 44.4 us
    ppermute x0 -> x7, waiting for transfers between devices: none -> 89.4 us  [the longest x4 88.2 us: ring_gather(): lax.ppermute(going_up, axis, [(d, (d + 1) % ways) for d in range(ways)])]
    all_gather x1 -> x0, waiting for transfers between devices: 76.9 us -> none  [body(): w_second = lax.all_gather(w_out[0], 'dp', axis=0, tiled=True)]
    all_gather x1, waiting for transfers between devices: 177 us -> 101 us  [body(): w_first = lax.all_gather(w_in[0], 'dp', axis=0, tiled=True)]
    ppermute x0 -> x7, starting transfers between devices: none -> 16 us  [the longest x3 8.13 us: ring_gather(): lax.ppermute(going_down, axis, [(d, (d - 1) % ways) for d in range(ways)])]
  transfers between devices with their start and end apart: 9 -> 15, of which waited for: 9 -> 13; matrix products, arithmetic and copies ran while one was open for 1% -> 2% of each run, Pallas kernels for 0% -> 0%
where the time goes in v1:
time: 830 us; the launch traced here: 828 us
  waiting for transfers between devices  648 us (78%)
  matrix products  70 us (8%)
  local copies, waits for them, and re-layouts  44.4 us (5%)
  other arithmetic  28.8 us (3%)
  starting transfers between devices  22.6 us (3%)
  between operations  13.8 us (2%)
    reduce_scatter x1, waiting for transfers between devices, body(): lax.psum_scatter(contract_rows(normed_rows, store).astype(jnp.bfloat16),...  209 us
    ppermute x5, waiting for transfers between devices, passed_along(): return lax.ppermute(shard, axis, pairs)  172 us
    all_gather x1, waiting for transfers between devices, body(): w_first = lax.all_gather(w_in[0], 'dp', axis=0, tiled=True)  101 us
    ppermute x4, waiting for transfers between devices, ring_gather(): lax.ppermute(going_up, axis, [(d, (d + 1) % ways) for d in range(ways)])  88.2 us
    reduce_scatter x1, waiting for transfers between devices, body(): lax.psum_scatter(acc_out.astype(jnp.bfloat16), 'dp', scatter_dimension=0,...  77.3 us
    dot_general x2, matrix products, layer_back(): lax.dot_general(grad_preact, w_first, (((1,), (1,)), ((), ())), preferred...  18.1 us
  transfers between devices with their start and end apart: 15, of which 13 were waited for; matrix products, arithmetic and copies ran while one was open for 2% of the time, Pallas kernels for 0%

profile of v1, /device:TPU:0, one launch (start us, length us, event | category | flops | bytes accessed | tf_op | source)
XLA Modules:
  0.0 828.5 jit_solution(17890933168850872709)
XLA Ops:
  14.1 29.9 %collective-permute-done.1 = bf16[128,2048]{1,0:T(8,128)(2,1)S(1)} collective-permute-done((bf16[128,2048]{1,0:T(8,128)(2,1)}, bf16[128,2048]{1,0:T(8,128)(2,1)S(1)}, u32[]{:S(2)}, u32[]{:S(2)}) %collective-permute-start.1) | collective-permute-done | bytes 524320 | tf_op jit(solution)/shard_map/ppermute | solution.py:18
  53.1 19.9 %collective-permute-done.3 = bf16[128,2048]{1,0:T(8,128)(2,1)S(1)} collective-permute-done((bf16[128,2048]{1,0:T(8,128)(2,1)S(1)}, bf16[128,2048]{1,0:T(8,128)(2,1)S(1)}, u32[]{:S(2)}, u32[]{:S(2)}) %collective-permute-start.3) | collective-permute-done | bytes 524320 | tf_op jit(solution)/shard_map/ppermute | solution.py:18
  81.0 20.9 %collective-permute-done.5 = bf16[128,2048]{1,0:T(8,128)(2,1)S(1)} collective-permute-done((bf16[128,2048]{1,0:T(8,128)(2,1)S(1)}, bf16[128,2048]{1,0:T(8,128)(2,1)S(1)}, u32[]{:S(2)}, u32[]{:S(2)}) %collective-permute-start.5) | collective-permute-done | bytes 524320 | tf_op jit(solution)/shard_map/ppermute | solution.py:18
  104.4 17.4 %collective-permute-done.7 = bf16[128,2048]{1,0:T(8,128)(2,1)S(1)} collective-permute-done((bf16[128,2048]{1,0:T(8,128)(2,1)S(1)}, bf16[128,2048]{1,0:T(8,128)(2,1)S(1)}, u32[]{:S(2)}, u32[]{:S(2)}) %collective-permute-start.7) | collective-permute-done | bytes 524320 | tf_op jit(solution)/shard_map/ppermute | solution.py:18
  122.7 100.6 %all-gather.3.cloned.1.call-done = bf16[1,2048,3072]{2,1,0:T(8,128)(2,1)} async-done(((bf16[1,256,3072]{2,1,0:T(8,128)(2,1)}), bf16[1,2048,3072]{2,1,0:T(8,128)(2,1)}) %all-gather.3.cloned.1.call-update) | async-done | bytes 12582928 | tf_op jit(solution)/shard_map/all_gather | solution.py:98
  225.5 4.3 broadcast_in_dim.60
  230.8 284.9 %while.21 = (s32[]{:T(128)}, bf16[128,2048]{1,0:T(8,128)(2,1)}, bf16[256,3072]{1,0:T(8,128)(2,1)}, f32[1024,2048]{1,0:T(8,128)}, bf16[256,2048]{1,0:T(8,128)(2,1...) while((s32[]{:T(128)}, bf16[128,2048]{1,0:T(8,128)(2,1)}, ...), condition=%wide.region_12.13_spmd, body=%wide.region_0.12_spmd.sunk | while | flops 4473488384 | bytes 157841232 | solution.py:142
  238.6 8.8 %collective-permute-done = bf16[128,2048]{1,0:T(8,128)(2,1)S(1)} collective-permute-done((bf16[128,2048]{1,0:T(8,128)(2,1)}, bf16[128,2048]{1,0:T(8,128)(2,1)S(1)}, u32[]{:S(2)}, u32[]{:S(2)}) %collective-permute-start) | collective-permute-done | bytes 524320 | tf_op jit(solution)/shard_map/while/body/eval_jaxpr/ppermute | solution.py:31
  250.4 148.2 %collective-permute-done = bf16[128,2048]{1,0:T(8,128)(2,1)S(1)} collective-permute-done((bf16[128,2048]{1,0:T(8,128)(2,1)}, bf16[128,2048]{1,0:T(8,128)(2,1)S(1)}, u32[]{:S(2)}, u32[]{:S(2)}) %collective-permute-start) | collective-permute-done | bytes 524320 | tf_op jit(solution)/shard_map/while/body/eval_jaxpr/ppermute | solution.py:31
  399.4 50.0 %conditional.2 = (bf16[128,2048]{1,0:T(8,128)(2,1)}, bf16[256,3072]{1,0:T(8,128)(2,1)}, f32[1024,2048]{1,0:T(8,128)}, bf16[256,2048]{1,0:T(8,128)(2,1)}) conditional(s32[]{:T(128)} %convert_element_type.154, (bf16[256,3072]{1,0:T(8,128)(2,1)}, f32[1024,2048]{1,0:T(8,128)}, bf16[256,2048]{1,0:T(8,128)(2,1)}) %tuple.69, (pred[]{:T(512)}, s32[]{:T(128)}, ...), branch_computations={%region_1.1_spmd, %region_2.11_spmd} | conditional | flops 4473488384 | bytes 153646560 | solution.py:132
  399.9 7.9 multiply_convert_fusion.1
  411.8 3.8 multiply_reduce_fusion
  433.6 9.0 %fusion.6 = (f32[128]{0:T(128)S(1)}, f32[128,2048]{1,0:T(8,128)S(1)}) fusion(f32[128]{0:T(128)S(1)} %broadcast_multiply_fusion.1, bf16[256,2048]{1,0:T(8,128)(2,1)S(1)} %get-tuple-element.374, s32[]{:T(128)S(6)} %select_n.83, bf16[128,3072]{1,0:T(8,128)(2,1)S(1)} %get-tuple-element.433, bf16[2048,3072]{1,0:T(8,128)(2,1)} %get-tuple-element.375), kind=kOutput, calls=%fused_computation.17 | convolution fusion | flops 1611661184 | bytes 14943236 | tf_op jit(solution)/shard_map/while/body/eval_jaxpr/cond/branch_1_fun/dot_general | solution.py:88
  450.7 9.4 %collective-permute-done = bf16[128,2048]{1,0:T(8,128)(2,1)S(1)} collective-permute-done((bf16[128,2048]{1,0:T(8,128)(2,1)}, bf16[128,2048]{1,0:T(8,128)(2,1)S(1)}, u32[]{:S(2)}, u32[]{:S(2)}) %collective-permute-start) | collective-permute-done | bytes 524320 | tf_op jit(solution)/shard_map/while/body/eval_jaxpr/ppermute | solution.py:31
  460.9 50.0 %conditional.2 = (bf16[128,2048]{1,0:T(8,128)(2,1)}, bf16[256,3072]{1,0:T(8,128)(2,1)}, f32[1024,2048]{1,0:T(8,128)}, bf16[256,2048]{1,0:T(8,128)(2,1)}) conditional(s32[]{:T(128)} %convert_element_type.154, (bf16[256,3072]{1,0:T(8,128)(2,1)}, f32[1024,2048]{1,0:T(8,128)}, bf16[256,2048]{1,0:T(8,128)(2,1)}) %tuple.69, (pred[]{:T(512)}, s32[]{:T(128)}, ...), branch_computations={%region_1.1_spmd, %region_2.11_spmd} | conditional | flops 4473488384 | bytes 153646560 | solution.py:132
  461.4 7.9 multiply_convert_fusion.1
  473.3 3.8 multiply_reduce_fusion
  495.1 9.0 %fusion.6 = (f32[128]{0:T(128)S(1)}, f32[128,2048]{1,0:T(8,128)S(1)}) fusion(f32[128]{0:T(128)S(1)} %broadcast_multiply_fusion.1, bf16[256,2048]{1,0:T(8,128)(2,1)S(1)} %get-tuple-element.374, s32[]{:T(128)S(6)} %select_n.83, bf16[128,3072]{1,0:T(8,128)(2,1)S(1)} %get-tuple-element.433, bf16[2048,3072]{1,0:T(8,128)(2,1)} %get-tuple-element.375), kind=kOutput, calls=%fused_computation.17 | convolution fusion | flops 1611661184 | bytes 14943236 | tf_op jit(solution)/shard_map/while/body/eval_jaxpr/cond/branch_1_fun/dot_general | solution.py:88
  507.7 3.2 copy-done
  515.8 6.0 convert_element_type.89
  522.5 8.0 convolution_convert_fusion
  530.5 77.3 %reduce-scatter.5.cloned.1.call-done = bf16[128,2048]{1,0:T(8,128)(2,1)} async-done(((bf16[1024,2048]{1,0:T(8,128)(2,1)}), bf16[128,2048]{1,0:T(8,128)(2,1)}) %reduce-scatter.5.cloned.1.call-update) | async-done | bytes 524304 | tf_op jit(solution)/shard_map/reduce_scatter | solution.py:150
  610.0 208.6 %reduce-scatter.3.cloned.1.call-done = bf16[256,3072]{1,0:T(8,128)(2,1)} async-done(((bf16[2048,3072]{1,0:T(8,128)(2,1)}), bf16[256,3072]{1,0:T(8,128)(2,1)}) %reduce-scatter.3.cloned.1.call-update) | async-done | bytes 1572880 | tf_op jit(solution)/shard_map/reduce_scatter | solution.py:144
  818.5 3.4 bitcast_convert_fusion
  (181 shorter events, 109.4 us)
Async XLA Ops:
  7.2 216.1 %all-gather.3.cloned.1.call-start = ((), (), s32[]{:S(2)}) async-start(), calls=%async_computation.4 | async-start | bytes 14155776 | tf_op jit(solution)/shard_map/all_gather | solution.py:98
  7.9 599.9 %reduce-scatter.5.cloned.1.call-start = ((), (), s32[]{:S(2)}) async-start(), calls=%async_computation.3 | async-start | bytes 4718592 | tf_op jit(solution)/shard_map/reduce_scatter | solution.py:150
  7.9 36.1 %collective-permute-start.1 = (bf16[128,2048]{1,0:T(8,128)(2,1)}, bf16[128,2048]{1,0:T(8,128)(2,1)S(1)}, u32[]{:S(2)}, u32[]{:S(2)}) collective-permute-start(bf16[128,2048]{1,0:T(8,128)(2,1)} %bitcast.78), channel_id=1, source_target_pairs={{0,1},{1,2},{2,3},{3,4},{4,5},{5,6},{6,7},{7,0},{8,9},{9,10},{10,1... | collective-permute-start | bytes 1572872 | tf_op jit(solution)/shard_map/ppermute | solution.py:18
  11.0 36.7 %collective-permute-start.2 = (bf16[128,2048]{1,0:T(8,128)(2,1)}, bf16[128,2048]{1,0:T(8,128)(2,1)S(1)}, u32[]{:S(2)}, u32[]{:S(2)}) collective-permute-start(bf16[128,2048]{1,0:T(8,128)(2,1)} %bitcast.79), channel_id=1, source_target_pairs={{0,7},{1,0},{2,1},{3,2},{4,3},{5,4},{6,5},{7,6},{8,15},{9,8},{10,9... | collective-permute-start | bytes 1572872 | tf_op jit(solution)/shard_map/ppermute | solution.py:21
  44.0 28.9 %collective-permute-start.3 = (bf16[128,2048]{1,0:T(8,128)(2,1)S(1)}, bf16[128,2048]{1,0:T(8,128)(2,1)S(1)}, u32[]{:S(2)}, u32[]{:S(2)}) collective-permute-start(bf16[128,2048]{1,0:T(8,128)(2,1)S(1)} %collective-permute-done.1), channel_id=1, source_target_pairs={{0,1},{1,2},{2,3},{3,4},{4,5},{5,6},{6,7},{7,0},{8,9},{9,10},{10,1... | collective-permute-start | bytes 1572872 | tf_op jit(solution)/shard_map/ppermute | solution.py:18
  46.4 5.8 copy-start.10
  47.7 29.5 %collective-permute-start.4 = (bf16[128,2048]{1,0:T(8,128)(2,1)S(1)}, bf16[128,2048]{1,0:T(8,128)(2,1)S(1)}, u32[]{:S(2)}, u32[]{:S(2)}) collective-permute-start(bf16[128,2048]{1,0:T(8,128)(2,1)S(1)} %collective-permute-done.2), channel_id=1, source_target_pairs={{0,7},{1,0},{2,1},{3,2},{4,3},{5,4},{6,5},{7,6},{8,15},{9,8},{10,9... | collective-permute-start | bytes 1572872 | tf_op jit(solution)/shard_map/ppermute | solution.py:21
  72.9 29.0 %collective-permute-start.5 = (bf16[128,2048]{1,0:T(8,128)(2,1)S(1)}, bf16[128,2048]{1,0:T(8,128)(2,1)S(1)}, u32[]{:S(2)}, u32[]{:S(2)}) collective-permute-start(bf16[128,2048]{1,0:T(8,128)(2,1)S(1)} %collective-permute-done.3), channel_id=1, source_target_pairs={{0,1},{1,2},{2,3},{3,4},{4,5},{5,6},{6,7},{7,0},{8,9},{9,10},{10,1... | collective-permute-start | bytes 1572872 | tf_op jit(solution)/shard_map/ppermute | solution.py:18
  77.2 26.5 %collective-permute-start.6 = (bf16[128,2048]{1,0:T(8,128)(2,1)S(1)}, bf16[128,2048]{1,0:T(8,128)(2,1)S(1)}, u32[]{:S(2)}, u32[]{:S(2)}) collective-permute-start(bf16[128,2048]{1,0:T(8,128)(2,1)S(1)} %collective-permute-done.4), channel_id=1, source_target_pairs={{0,7},{1,0},{2,1},{3,2},{4,3},{5,4},{6,5},{7,6},{8,15},{9,8},{10,9... | collective-permute-start | bytes 1572872 | tf_op jit(solution)/shard_map/ppermute | solution.py:21
  101.9 19.9 %collective-permute-start.7 = (bf16[128,2048]{1,0:T(8,128)(2,1)S(1)}, bf16[128,2048]{1,0:T(8,128)(2,1)S(1)}, u32[]{:S(2)}, u32[]{:S(2)}) collective-permute-start(bf16[128,2048]{1,0:T(8,128)(2,1)S(1)} %collective-permute-done.5), channel_id=1, source_target_pairs={{0,1},{1,2},{2,3},{3,4},{4,5},{5,6},{6,7},{7,0},{8,9},{9,10},{10,1... | collective-permute-start | bytes 1572872 | tf_op jit(solution)/shard_map/ppermute | solution.py:18
  231.7 4.0 collective-permute-start
  237.3 10.1 %collective-permute-start = (bf16[128,2048]{1,0:T(8,128)(2,1)}, bf16[128,2048]{1,0:T(8,128)(2,1)S(1)}, u32[]{:S(2)}, u32[]{:S(2)}) collective-permute-start(bf16[128,2048]{1,0:T(8,128)(2,1)} %get-tuple-element.526), channel_id=1, source_target_pairs={{8,0},{16,8},{24,16},{9,1},{17,9},{25,17},{10,2},{18,10},{26,18},{... | collective-permute-start | bytes 1572872 | tf_op jit(solution)/shard_map/while/body/eval_jaxpr/ppermute | solution.py:31
  249.1 149.5 %collective-permute-start = (bf16[128,2048]{1,0:T(8,128)(2,1)}, bf16[128,2048]{1,0:T(8,128)(2,1)S(1)}, u32[]{:S(2)}, u32[]{:S(2)}) collective-permute-start(bf16[128,2048]{1,0:T(8,128)(2,1)} %get-tuple-element.526), channel_id=1, source_target_pairs={{8,0},{16,8},{24,16},{9,1},{17,9},{25,17},{10,2},{18,10},{26,18},{... | collective-permute-start | bytes 1572872 | tf_op jit(solution)/shard_map/while/body/eval_jaxpr/ppermute | solution.py:31
  399.8 7.9 copy-start.11
  433.6 10.9 %slice-start = ((s8[8388608]{0:T(1024)(128)(4,1)}), s8[4194304]{0:T(1024)(128)(4,1)S(1)}, s32[]{:S(2)}) async-start(s8[8388608]{0:T(1024)(128)(4,1)} %bitcast.59), calls=%async_computation.5 | async-start | bytes 8388608 | tf_op jit(solution)/shard_map/while/body/eval_jaxpr/cond
  433.6 9.0 %copy-start.12 = (f32[128]{0:T(128)S(1)}, f32[128]{0:T(128)}, u32[]{:S(2)}) copy-start(f32[128]{0:T(128)} %copy-done.11) | copy-start | bytes 1540 | tf_op jit(solution)/shard_map/while/body/eval_jaxpr/cond
  433.6 10.9 %slice-start.1 = ((s8[8388608]{0:T(1024)(128)(4,1)}), s8[4194304]{0:T(1024)(128)(4,1)S(1)}, s32[]{:S(2)}) async-start(s8[8388608]{0:T(1024)(128)(4,1)} %bitcast.59), calls=%async_computation.6 | async-start | bytes 8388608 | tf_op jit(solution)/shard_map/while/body/eval_jaxpr/cond
  449.4 10.7 %collective-permute-start = (bf16[128,2048]{1,0:T(8,128)(2,1)}, bf16[128,2048]{1,0:T(8,128)(2,1)S(1)}, u32[]{:S(2)}, u32[]{:S(2)}) collective-permute-start(bf16[128,2048]{1,0:T(8,128)(2,1)} %get-tuple-element.526), channel_id=1, source_target_pairs={{8,0},{16,8},{24,16},{9,1},{17,9},{25,17},{10,2},{18,10},{26,18},{... | collective-permute-start | bytes 1572872 | tf_op jit(solution)/shard_map/while/body/eval_jaxpr/ppermute | solution.py:31
  461.4 7.9 copy-start.11
  495.1 10.9 %slice-start = ((s8[8388608]{0:T(1024)(128)(4,1)}), s8[4194304]{0:T(1024)(128)(4,1)S(1)}, s32[]{:S(2)}) async-start(s8[8388608]{0:T(1024)(128)(4,1)} %bitcast.59), calls=%async_computation.5 | async-start | bytes 8388608 | tf_op jit(solution)/shard_map/while/body/eval_jaxpr/cond
  495.1 9.0 %copy-start.12 = (f32[128]{0:T(128)S(1)}, f32[128]{0:T(128)}, u32[]{:S(2)}) copy-start(f32[128]{0:T(128)} %copy-done.11) | copy-start | bytes 1540 | tf_op jit(solution)/shard_map/while/body/eval_jaxpr/cond
  495.1 10.9 %slice-start.1 = ((s8[8388608]{0:T(1024)(128)(4,1)}), s8[4194304]{0:T(1024)(128)(4,1)S(1)}, s32[]{:S(2)}) async-start(s8[8388608]{0:T(1024)(128)(4,1)} %bitcast.59), calls=%async_computation.6 | async-start | bytes 8388608 | tf_op jit(solution)/shard_map/while/body/eval_jaxpr/cond
  510.9 4.0 collective-permute-start
  521.8 296.7 %reduce-scatter.3.cloned.1.call-start = ((), (), s32[]{:S(2)}) async-start(), calls=%async_computation.2 | async-start | bytes 14155776 | tf_op jit(solution)/shard_map/reduce_scatter | solution.py:144
  (22 other events, 41.0 us)
Sparse Core Ops, SparseCore 0:
  10.2 213.0 all-gather.2
  521.9 85.8 reduce-scatter.4
  611.4 207.0 reduce-scatter.2
